TPU v7x, 32 devices: a whole 2x2x4 slice. The times are simulated.
32 devices in a mesh: parts: 2 (over y), expert: 8 (over z, x), dp: 2 (over core).
Axes of the slice: x: 2, y: 2, z: 4, core: 2. Of those that a mesh axis runs over, the one named last changes fastest.
Arguments:
- tokens: bfloat16 [4096, 2048], P(('parts', 'expert', 'dp')), parts along dimension 0, may hold values from -6 to 6
- route_ids: int32 [4096, 2], P(('parts', 'expert', 'dp')), parts along dimension 0, may hold values from 0 to 31, all different within a row; in each aligned block of 128 rows (0 to 127, 128 to 255, ...) at most 10 rows name the same one
- route_gates: float32 [4096, 2], P(('parts', 'expert', 'dp')), parts along dimension 0, may hold values from 0.1 to 1
- gate_weight: bfloat16 [32, 2048, 1408], P('expert', None, 'dp'), may hold values from -0.125 to 0.125
- up_weight: bfloat16 [32, 2048, 1408], P('expert', None, 'dp'), may hold values from -0.125 to 0.125
- down_weight: bfloat16 [32, 1408, 2048], P('expert'), may hold values from -0.15625 to 0.15625
Outputs:
- output: bfloat16 [4096, 2048], P(('parts', 'expert', 'dp')), parts along dimension 0
There are 2 independent parts, one for each index of `parts`. A program takes and returns all parts, laid end to end along the dimension named above; an argument that names none is the same for every part. Nothing has to cross between parts.
Inputs may be any that keep to these rules, and one draw needn't show every extreme that they name: `route_ids`: each row names 2 different experts; within the rows of one device (aligned blocks of 128 rows) no expert is named by more than 10 rows, a bound that some block reaches.
All inputs are finite; a program needn't handle non-finite values.
Results may differ from a plain program's by a relative error of at most 0.0058.
Values may be sent and summed in bfloat16 or wider, within the bound.
No kernel may reach another device: no remote copies, remote signals or barrier semaphores. Data moves between devices by JAX's collectives and lax.ppermute only.
A program may use at most 192 MiB of HBM per device.

v0:
```python
import jax
import jax.numpy as jnp
from jax import lax
from jax.sharding import PartitionSpec as P

FF = 1408
EXPERTS = 32
CAP = 10


def on_device(tokens, route_ids, route_gates, gate_weight, up_weight, down_weight):
    row_count = tokens.shape[0]
    width = tokens.shape[1]
    local_segs = gate_weight.shape[0]
    seg_width = down_weight.shape[1]
    groups = lax.axis_size("expert")
    per_expert = FF // seg_width
    expert_iota = jnp.arange(EXPERTS, dtype=jnp.int32)
    matched = route_ids[:, :, None] == expert_iota[None, None, :]
    member = jnp.sum(matched.astype(jnp.int32), axis=1)
    weighting = jnp.sum(jnp.where(matched, route_gates[:, :, None], jnp.float32(0.0)), axis=1)
    ranking = jnp.cumsum(member, axis=0) - member
    slot_iota = jnp.arange(CAP, dtype=jnp.int32)
    placed = (member[:, :, None] == 1) & (ranking[:, :, None] == slot_iota[None, None, :])
    placed_flat = placed.reshape(row_count, EXPERTS * CAP)
    chooser = placed_flat.astype(jnp.bfloat16)
    packed = jnp.dot(chooser.T, tokens, preferred_element_type=jnp.float32).astype(jnp.bfloat16)
    packed_four = packed.reshape(EXPERTS, 1, CAP, width)
    outgoing = jnp.broadcast_to(packed_four, (EXPERTS, per_expert, CAP, width))
    outgoing = outgoing.reshape(groups, local_segs, CAP, width)
    incoming = lax.all_to_all(outgoing, "expert", split_axis=0, concat_axis=0, tiled=True)
    full_gate, full_up = (
        lax.all_gather(gate_weight, "dp", axis=2, tiled=True),
        lax.all_gather(up_weight, "dp", axis=2, tiled=True),
    )
    gate_val = jnp.einsum("gscd,sdf->gscf", incoming, full_gate, preferred_element_type=jnp.float32)
    up_val = jnp.einsum("gscd,sdf->gscf", incoming, full_up, preferred_element_type=jnp.float32)
    hidden = (jax.nn.silu(gate_val) * up_val).astype(jnp.bfloat16)
    partial_value = jnp.einsum(
        "gscf,sfd->gscd", hidden, down_weight, preferred_element_type=jnp.float32
    ).astype(jnp.bfloat16)
    returned = lax.all_to_all(partial_value, "expert", split_axis=0, concat_axis=0, tiled=True)
    per_seg = returned.reshape(EXPERTS, per_expert, CAP, width).astype(jnp.float32)
    expert_out = jnp.sum(per_seg, axis=1).reshape(EXPERTS * CAP, width)
    combine = jnp.where(placed, weighting[:, :, None], jnp.float32(0.0)).reshape(
        row_count, EXPERTS * CAP
    )
    output = jnp.dot(
        combine, expert_out, precision=lax.Precision.HIGHEST, preferred_element_type=jnp.float32
    )
    return output.astype(jnp.bfloat16)


def solution(mesh):
    placed = (
        P(("parts", "expert", "dp"), None),
        P(("parts", "expert", "dp"), None),
        P(("parts", "expert", "dp"), None),
        P("expert", None, "dp"),
        P("expert", None, "dp"),
        P("expert", None, None),
    )
    return jax.shard_map(
        on_device,
        mesh=mesh,
        in_specs=placed,
        out_specs=P(("parts", "expert", "dp"), None),
        check_vma=False,
    )
```

profile of v0, /device:TPU:0, one launch (start us, length us, event | category | flops | bytes accessed | tf_op | source)
XLA Modules:
  0.0 167.0 jit_solution(10947640230947168460)
XLA Ops:
  6.5 0.0 copy-start
  6.5 0.0 all-gather.3.cloned.1.call-start
  6.5 0.7 all-gather.3.cloned.1.call-update
  7.3 0.0 copy-start.2
  7.3 0.0 all-gather.5.cloned.1.call-start
  7.3 0.7 all-gather.5.cloned.1.call-update
  8.0 0.0 copy-done.2
  8.0 0.1 copy.25
  8.1 0.2 reduce_window_sum.11
  8.3 0.1 copy.27
  8.6 0.1 eq.66
  8.7 0.0 copy-done
  8.7 1.6 convolution_convert_fusion
  10.3 2.3 %reshape_reshape.3 = bf16[8,4,10,2048]{3,2,1,0:T(8,128)(2,1)S(1)} reshape(bf16[320,2048]{1,0:T(8,128)(2,1)} %convolution_convert_fusion) | data formatting | bytes 2621440 | tf_op jit(solution)/shard_map/reshape;reshape | solution.py:30
  12.6 1.0 copy.28
  13.6 38.4 %all_to_all.10 = bf16[8,4,10,2048]{3,1,2,0:T(4,128)(2,1)S(1)} all-to-all(bf16[8,4,10,2048]{3,1,2,0:T(4,128)(2,1)S(1)} %copy.28), channel_id=1, replica_groups=mesh['parts'=2,'expert'=8,'dp'=2] {'expert'}, dimensions={0} | all-to-all | bytes 2621440 | tf_op jit(solution)/shard_map/all_to_all | solution.py:31
  52.1 0.0 all-gather.3.cloned.1.call-done
  52.1 15.3 %fusion.6 = f32[8,4,10,1408]{3,2,0,1:T(8,128)} fusion(bf16[4,2048,1408]{1,2,0:T(8,128)(2,1)} %all-gather.3.cloned.1.call-done, bf16[8,4,10,2048]{3,1,2,0:T(4,128)(2,1)S(1)} %all_to_all.10), kind=kOutput, calls=%fused_computation.6 | convolution fusion | flops 1845493760 | bytes 26181632 | tf_op jit(solution)/shard_map/gscd,sdf->gscf/dot_general | solution.py:36
  67.3 22.3 %all-gather.5.cloned.1.call-done = bf16[4,2048,1408]{1,2,0:T(8,128)(2,1)} async-done(((bf16[4,2048,704]{1,2,0:T(8,128)(2,1)}), bf16[4,2048,1408]{1,2,0:T(8,128)(2,1)}) %all-gather.5.cloned.1.call-update) | async-done | bytes 23068688 | tf_op jit(solution)/shard_map/all_gather | solution.py:34
  89.6 12.9 %fusion.15 = bf16[8,4,10,1408]{3,2,0,1:T(8,128)(2,1)S(1)} fusion(bf16[4,2048,1408]{1,2,0:T(8,128)(2,1)} %all-gather.5.cloned.1.call-done, f32[8,4,10,1408]{3,2,0,1:T(8,128)} %fusion.6, bf16[8,4,10,2048]{3,1,2,0:T(4,128)(2,1)S(1)} %all_to_all.10), kind=kOutput, calls=%fused_computation.9 | convolution fusion | flops 1848197120 | bytes 27082752 | tf_op jit(solution)/shard_map/gscd,sdf->gscf/dot_general | solution.py:37
  102.6 11.0 %fusion.21 = bf16[8,4,10,2048]{3,2,0,1:T(8,128)(2,1)S(1)} fusion(bf16[8,4,10,1408]{3,2,0,1:T(8,128)(2,1)S(1)} %fusion.15, bf16[4,1408,2048]{2,1,0:T(8,128)(2,1)} %param.11), kind=kOutput, calls=%fused_computation.11 | convolution fusion | flops 1846149120 | bytes 25280512 | tf_op jit(solution)/shard_map/gscf,sfd->gscd/dot_general | solution.py:39
  113.6 0.0 copy-start.3
  113.6 2.1 %copy.31 = bf16[8,4,10,2048]{3,1,2,0:T(4,128)(2,1)} copy(bf16[8,4,10,2048]{3,2,0,1:T(8,128)(2,1)S(1)} %fusion.21) | data formatting | bytes 2621440 | tf_op jit(solution)/shard_map/convert_element_type | solution.py:41
  115.7 5.8 %all-to-all-start.1 = ((bf16[8,4,10,2048]{3,1,2,0:T(4,128)(2,1)}), bf16[8,4,10,2048]{3,1,2,0:T(4,128)(2,1)}, u32[]{:S(2)}, u32[]{:S(2)}) async-start(bf16[8,4,10,2048]{3,1,2,0:T(4,128)(2,1)} %copy.31), calls=%async_computation.1 | async-start | bytes 2621440 | tf_op jit(solution)/shard_map/all_to_all | solution.py:42
  121.5 0.0 copy-done.3
  121.5 0.1 fusion.27
  121.6 31.8 %all-to-all-done.1 = bf16[8,4,10,2048]{3,1,2,0:T(4,128)(2,1)} async-done(((bf16[8,4,10,2048]{3,1,2,0:T(4,128)(2,1)}), bf16[8,4,10,2048]{3,1,2,0:T(4,128)(2,1)}, u32[]{:S(2)}, u32[]{:S(2)}) %all-to-all-start.1) | async-done | bytes 1310752 | tf_op jit(solution)/shard_map/all_to_all | solution.py:42
  153.4 0.0 copy-start.1
  153.4 2.3 %copy.32 = bf16[8,4,10,2048]{3,2,1,0:T(8,128)(2,1)S(1)} copy(bf16[8,4,10,2048]{3,1,2,0:T(4,128)(2,1)} %all-to-all-done.1) | data formatting | bytes 2621440 | tf_op jit(solution)/shard_map/all_to_all | solution.py:42
  155.7 1.3 reshape.68
  157.0 3.1 %convolution_convert_fusion.1 = bf16[128,2048]{1,0:T(8,128)(2,1)} fusion(f32[128,320]{0,1:T(8,128)S(1)} %select_n.20, bf16[320,2048]{1,0:T(8,128)(2,1)} %reshape.68), kind=kOutput, calls=%fused_computation.13 | convolution fusion | flops 1006895104 | bytes 1998848 | tf_op jit(solution)/shard_map/dot_general | solution.py:48
  160.1 0.0 copy-done.1
  (10 shorter events, 0.2 us)
Async XLA Ops:
  6.5 2.1 %copy-start = (bf16[128,2048]{1,0:T(8,128)(2,1)S(1)}, bf16[128,2048]{1,0:T(8,128)(2,1)}, u32[]{:S(2)}) copy-start(bf16[128,2048]{1,0:T(8,128)(2,1)} %param.6) | copy-start | bytes 1572868
  6.5 45.6 %all-gather.3.cloned.1.call-start = ((), (), s32[]{:S(2)}) async-start(), calls=%async_computation.2 | async-start | bytes 34603008 | tf_op jit(solution)/shard_map/all_gather | solution.py:33
  7.3 0.8 copy-start.2
  7.3 82.4 %all-gather.5.cloned.1.call-start = ((), (), s32[]{:S(2)}) async-start(), calls=%async_computation.3 | async-start | bytes 34603008 | tf_op jit(solution)/shard_map/all_gather | solution.py:34
  113.6 7.9 %copy-start.3 = (f32[128,2]{0,1:T(2,128)S(1)}, f32[128,2]{0,1:T(2,128)}, u32[]{:S(2)}) copy-start(f32[128,2]{0,1:T(2,128)} %param.8) | copy-start | bytes 3076
  115.7 37.7 %all-to-all-start.1 = ((bf16[8,4,10,2048]{3,1,2,0:T(4,128)(2,1)}), bf16[8,4,10,2048]{3,1,2,0:T(4,128)(2,1)}, u32[]{:S(2)}, u32[]{:S(2)}) async-start(bf16[8,4,10,2048]{3,1,2,0:T(4,128)(2,1)} %copy.31), calls=%async_computation.1 | async-start | bytes 2621440 | tf_op jit(solution)/shard_map/all_to_all | solution.py:42
  153.4 6.7 %copy-start.1 = (bf16[128,2048]{1,0:T(8,128)(2,1)S(1)}, bf16[128,2048]{1,0:T(8,128)(2,1)}, u32[]{:S(2)}) copy-start(bf16[128,2048]{1,0:T(8,128)(2,1)} %param.6) | copy-start | bytes 1572868
Sparse Core Ops, SparseCore 0:
  8.9 40.3 all-gather.2
  50.8 38.7 all-gather.4
where the time goes:
time: 167 us
  waiting for transfers between devices  55.5 us (33%)
  matrix products  43.9 us (26%)
  blocking collectives  38.4 us (23%)
  between operations  13.6 us (8%)
  local copies, waits for them, and re-layouts  9.43 us (6%)
  starting transfers between devices  5.81 us (3%)
    all_to_all x1, blocking collectives, on_device(): lax.all_to_all(outgoing, 'expert', split_axis=0, concat_axis=0, tiled=True)  38.4 us
    all_to_all x1, waiting for transfers between devices, on_device(): lax.all_to_all(partial_value, 'expert', split_axis=0, concat_axis=0, tile...  31.8 us
    all_gather x1, waiting for transfers between devices, on_device(): lax.all_gather(up_weight, 'dp', axis=2, tiled=True)  22.3 us
    dot_general x1, matrix products, on_device(): jnp.einsum('gscd,sdf->gscf', incoming, full_gate, preferred_element_type=...  15.3 us
    dot_general x1, matrix products, on_device(): jnp.einsum('gscd,sdf->gscf', incoming, full_up, preferred_element_type=jn...  12.9 us
    dot_general x1, matrix products, on_device(): jnp.einsum('gscf,sfd->gscd', hidden, down_weight, preferred_element_type=...  11 us
    all_to_all x1, starting transfers between devices, on_device(): lax.all_to_all(partial_value, 'expert', split_axis=0, concat_axis=0, tile...  5.77 us
  transfers between devices with their start and end apart: 3, of which 2 were waited for; matrix products, arithmetic and copies ran while one was open for 13% of the time, Pallas kernels for 0%

commit v1 on v0

--- a/solution.py
+++ b/solution.py
@@ -6,6 +6,25 @@
 FF = 1408
 EXPERTS = 32
 CAP = 10
+
+
+def _perform_hubs(piece_in, at_axis, along_dim):
+    finding, y = (lax.axis_size("expert"), lax.axis_index("expert"))
+    clean = list(piece_in.shape)
+    local_now = piece_in.shape[at_axis] // finding
+    clean[at_axis] = local_now
+    top = clean[along_dim]
+    clean[along_dim] = top * finding
+    tall = jnp.zeros(clean, piece_in.dtype)
+    for s in range(finding):
+        b_next = lax.dynamic_slice_in_dim(piece_in, (y ^ s) * local_now, local_now, axis=at_axis)
+        if s:
+            x_next = range(finding)
+            t_next = map(lambda dev_i: (dev_i, dev_i ^ s), x_next)
+            right_arr = list(t_next)
+            b_next = lax.ppermute(b_next, axis_name="expert", perm=right_arr)
+        tall = lax.dynamic_update_slice_in_dim(tall, b_next, (y ^ s) * top, axis=along_dim)
+    return tall
 
 
 def on_device(tokens, route_ids, route_gates, gate_weight, up_weight, down_weight):
@@ -39,7 +58,7 @@
     partial_value = jnp.einsum(
         "gscf,sfd->gscd", hidden, down_weight, preferred_element_type=jnp.float32
     ).astype(jnp.bfloat16)
-    returned = lax.all_to_all(partial_value, "expert", split_axis=0, concat_axis=0, tiled=True)
+    returned = _perform_hubs(partial_value, 0, 0)
     per_seg = returned.reshape(EXPERTS, per_expert, CAP, width).astype(jnp.float32)
     expert_out = jnp.sum(per_seg, axis=1).reshape(EXPERTS * CAP, width)
     combine = jnp.where(placed, weighting[:, :, None], jnp.float32(0.0)).reshape(

time: 167 us -> 176 us (1.054)
  the two profiles are of different devices: /device:TPU:0 before, /device:TPU:16 now
where the time goes in v1:
time: 176 us
  waiting for transfers between devices  97.7 us (56%)
  matrix products  43.3 us (25%)
  starting transfers between devices  14.5 us (8%)
  between operations  13.6 us (8%)
  local copies, waits for them, and re-layouts  6.8 us (4%)
    ppermute x7, waiting for transfers between devices, _perform_hubs(): b_next = lax.ppermute(b_next, axis_name='expert', perm=right_arr)  43.8 us
    all_to_all x1, waiting for transfers between devices, on_device(): lax.all_to_all(outgoing, 'expert', split_axis=0, concat_axis=0, tiled=True)  28 us
    all_gather x1, waiting for transfers between devices, on_device(): lax.all_gather(up_weight, 'dp', axis=2, tiled=True)  24.5 us
    dot_general x1, matrix products, on_device(): jnp.einsum('gscd,sdf->gscf', incoming, full_gate, preferred_element_type=...  14.6 us
    dot_general x1, matrix products, on_device(): jnp.einsum('gscd,sdf->gscf', incoming, full_up, preferred_element_type=jn...  12.9 us
    dot_general x1, matrix products, on_device(): jnp.einsum('gscf,sfd->gscd', hidden, down_weight, preferred_element_type=...  11 us
    ppermute x7, starting transfers between devices, _perform_hubs(): b_next = lax.ppermute(b_next, axis_name='expert', perm=right_arr)  8.14 us
    all_to_all x1, starting transfers between devices, on_device(): lax.all_to_all(outgoing, 'expert', split_axis=0, concat_axis=0, tiled=True)  6.27 us
  transfers between devices with their start and end apart: 10, of which 8 were waited for; matrix products, arithmetic and copies ran while one was open for 12% of the time, Pallas kernels for 0%

profile of v1, /device:TPU:16, one launch (start us, length us, event | category | flops | bytes accessed | tf_op | source)
XLA Modules:
  0.0 176.2 jit_solution(11448239106916631537)
XLA Ops:
  6.5 0.7 all-gather.3.cloned.1.call-update
  7.3 0.7 all-gather.5.cloned.1.call-update
  8.0 0.1 copy.22
  8.1 0.2 reduce_window_sum.11
  8.6 0.1 eq.66
  8.7 1.6 convolution_convert_fusion
  10.3 2.3 %reshape_reshape.3 = bf16[8,4,10,2048]{3,2,1,0:T(8,128)(2,1)S(1)} reshape(bf16[320,2048]{1,0:T(8,128)(2,1)} %convolution_convert_fusion) | data formatting | bytes 2621440 | tf_op jit(solution)/shard_map/reshape;reshape | solution.py:49
  12.6 2.1 %copy.25 = bf16[8,4,10,2048]{3,1,2,0:T(4,128)(2,1)} copy(bf16[8,4,10,2048]{3,2,1,0:T(8,128)(2,1)S(1)} %reshape_reshape.3) | data formatting | bytes 2621440 | tf_op jit(solution)/shard_map/reshape;reshape | solution.py:49
  14.8 6.3 %all-to-all-start = ((bf16[8,4,10,2048]{3,1,2,0:T(4,128)(2,1)}), bf16[8,4,10,2048]{3,1,2,0:T(4,128)(2,1)S(1)}, u32[]{:S(2)}, u32[]{:S(2)}) async-start(bf16[8,4,10,2048]{3,1,2,0:T(4,128)(2,1)} %copy.25), calls=%async_computation | async-start | bytes 2621440 | tf_op jit(solution)/shard_map/all_to_all | solution.py:50
  21.0 0.1 fusion.24
  21.2 28.0 %all-to-all-done = bf16[8,4,10,2048]{3,1,2,0:T(4,128)(2,1)S(1)} async-done(((bf16[8,4,10,2048]{3,1,2,0:T(4,128)(2,1)}), bf16[8,4,10,2048]{3,1,2,0:T(4,128)(2,1)S(1)}, u32[]{:S(2)}, u32[]{:S(2)}) %all-to-all-start) | async-done | bytes 1310752 | tf_op jit(solution)/shard_map/all_to_all | solution.py:50
  49.1 14.6 %fusion.6 = f32[8,4,10,1408]{3,2,0,1:T(8,128)} fusion(bf16[4,2048,1408]{1,2,0:T(8,128)(2,1)} %all-gather.3.cloned.1.call-done, bf16[8,4,10,2048]{3,1,2,0:T(4,128)(2,1)S(1)} %all-to-all-done), kind=kOutput, calls=%fused_computation.6 | convolution fusion | flops 1845493760 | bytes 26181632 | tf_op jit(solution)/shard_map/gscd,sdf->gscf/dot_general | solution.py:55
  63.7 24.5 %all-gather.5.cloned.1.call-done = bf16[4,2048,1408]{1,2,0:T(8,128)(2,1)} async-done(((bf16[4,2048,704]{1,2,0:T(8,128)(2,1)}), bf16[4,2048,1408]{1,2,0:T(8,128)(2,1)}) %all-gather.5.cloned.1.call-update) | async-done | bytes 23068688 | tf_op jit(solution)/shard_map/all_gather | solution.py:53
  88.3 12.9 %fusion.15 = bf16[8,4,10,1408]{3,2,0,1:T(8,128)(2,1)S(1)} fusion(bf16[4,2048,1408]{1,2,0:T(8,128)(2,1)} %all-gather.5.cloned.1.call-done, f32[8,4,10,1408]{3,2,0,1:T(8,128)} %fusion.6, bf16[8,4,10,2048]{3,1,2,0:T(4,128)(2,1)S(1)} %all-to-all-done), kind=kOutput, calls=%fused_computation.9 | convolution fusion | flops 1848197120 | bytes 27082752 | tf_op jit(solution)/shard_map/gscd,sdf->gscf/dot_general | solution.py:56
  101.2 11.0 %fusion.18 = bf16[4,8,10,2048]{3,2,1,0:T(8,128)(2,1)S(1)} fusion(bf16[8,4,10,1408]{3,2,0,1:T(8,128)(2,1)S(1)} %fusion.15, bf16[4,1408,2048]{2,1,0:T(8,128)(2,1)} %param.11), kind=kOutput, calls=%fused_computation.10 | convolution fusion | flops 1846149120 | bytes 25280512 | tf_op jit(solution)/shard_map/gscf,sfd->gscd/dot_general | solution.py:58
  112.2 0.2 dynamic-slice_bitcast_fusion
  112.4 1.5 collective-permute-start
  114.0 1.5 collective-permute-start.1
  115.5 0.5 collective-permute-start.2
  116.0 0.3 collective-permute-start.3
  116.2 3.6 %collective-permute-start.4 = (bf16[1,4,10,2048]{3,2,1,0:T(8,128)(2,1)S(1)}, bf16[1,4,10,2048]{3,2,1,0:T(8,128)(2,1)S(1)}, u32[]{:S(2)}, u32[]{:S(2)}) collective-permute-start(bf16[1,4,10,2048]{3,2,1,0:T(8,128)(2,1)S(1)} %get-tuple-element.7), channel_id=1, source_target_pairs={{0,10},{2,8},{4,14},{6,12},{8,2},{10,0},{12,6},{14,4},{1,11},{3,9}... | collective-permute-start | bytes 491528 | tf_op jit(solution)/shard_map/ppermute | solution.py:25
  119.8 0.2 broadcast_in_dim.38
  120.1 0.9 collective-permute-done
  121.0 0.5 collective-permute-start.5
  121.6 9.5 %collective-permute-done.1 = bf16[1,4,10,2048]{3,2,1,0:T(8,128)(2,1)S(1)} collective-permute-done((bf16[1,4,10,2048]{3,2,1,0:T(8,128)(2,1)S(1)}, bf16[1,4,10,2048]{3,2,1,0:T(8,128)(2,1)S(1)}, u32[]{:S(2)}, u32[]{:S(2)}) %collective-permute-start.1) | collective-permute-done | bytes 163872 | tf_op jit(solution)/shard_map/ppermute | solution.py:25
  131.0 0.2 collective-permute-start.6
  131.3 4.4 %collective-permute-done.2 = bf16[1,4,10,2048]{3,2,1,0:T(8,128)(2,1)S(1)} collective-permute-done((bf16[1,4,10,2048]{3,2,1,0:T(8,128)(2,1)S(1)}, bf16[1,4,10,2048]{3,2,1,0:T(8,128)(2,1)S(1)}, u32[]{:S(2)}, u32[]{:S(2)}) %collective-permute-start.2) | collective-permute-done | bytes 163872 | tf_op jit(solution)/shard_map/ppermute | solution.py:25
  135.8 15.3 %collective-permute-done.4 = bf16[1,4,10,2048]{3,2,1,0:T(8,128)(2,1)S(1)} collective-permute-done((bf16[1,4,10,2048]{3,2,1,0:T(8,128)(2,1)S(1)}, bf16[1,4,10,2048]{3,2,1,0:T(8,128)(2,1)S(1)}, u32[]{:S(2)}, u32[]{:S(2)}) %collective-permute-start.4) | collective-permute-done | bytes 163872 | tf_op jit(solution)/shard_map/ppermute | solution.py:25
  151.1 8.7 %collective-permute-done.5 = bf16[1,4,10,2048]{3,2,1,0:T(8,128)(2,1)S(1)} collective-permute-done((bf16[1,4,10,2048]{3,2,1,0:T(8,128)(2,1)S(1)}, bf16[1,4,10,2048]{3,2,1,0:T(8,128)(2,1)S(1)}, u32[]{:S(2)}, u32[]{:S(2)}) %collective-permute-start.5) | collective-permute-done | bytes 163872 | tf_op jit(solution)/shard_map/ppermute | solution.py:25
  159.9 5.0 %collective-permute-done.6 = bf16[1,4,10,2048]{3,2,1,0:T(8,128)(2,1)S(1)} collective-permute-done((bf16[1,4,10,2048]{3,2,1,0:T(8,128)(2,1)S(1)}, bf16[1,4,10,2048]{3,2,1,0:T(8,128)(2,1)S(1)}, u32[]{:S(2)}, u32[]{:S(2)}) %collective-permute-start.6) | collective-permute-done | bytes 163872 | tf_op jit(solution)/shard_map/ppermute | solution.py:25
  164.9 1.3 reshape.76
  166.2 3.1 %convolution_convert_fusion.1 = bf16[128,2048]{1,0:T(8,128)(2,1)} fusion(f32[128,320]{0,1:T(8,128)S(1)} %select_n.52, bf16[320,2048]{1,0:T(8,128)(2,1)} %reshape.76), kind=kOutput, calls=%fused_computation.12 | convolution fusion | flops 1006895104 | bytes 1998848 | tf_op jit(solution)/shard_map/dot_general | solution.py:67
  (31 shorter events, 0.5 us)
Async XLA Ops:
  6.5 2.1 %copy-start = (bf16[128,2048]{1,0:T(8,128)(2,1)S(1)}, bf16[128,2048]{1,0:T(8,128)(2,1)}, u32[]{:S(2)}) copy-start(bf16[128,2048]{1,0:T(8,128)(2,1)} %param.6) | copy-start | bytes 1572868
  6.5 42.6 %all-gather.3.cloned.1.call-start = ((), (), s32[]{:S(2)}) async-start(), calls=%async_computation.1 | async-start | bytes 34603008 | tf_op jit(solution)/shard_map/all_gather | solution.py:52
  7.3 0.8 copy-start.2
  7.3 81.0 %all-gather.5.cloned.1.call-start = ((), (), s32[]{:S(2)}) async-start(), calls=%async_computation.2 | async-start | bytes 34603008 | tf_op jit(solution)/shard_map/all_gather | solution.py:53
  14.8 6.3 %copy-start.3 = (f32[128,2]{0,1:T(2,128)S(1)}, f32[128,2]{0,1:T(2,128)}, u32[]{:S(2)}) copy-start(f32[128,2]{0,1:T(2,128)} %param.8) | copy-start | bytes 3076
  14.8 34.4 %all-to-all-start = ((bf16[8,4,10,2048]{3,1,2,0:T(4,128)(2,1)}), bf16[8,4,10,2048]{3,1,2,0:T(4,128)(2,1)S(1)}, u32[]{:S(2)}, u32[]{:S(2)}) async-start(bf16[8,4,10,2048]{3,1,2,0:T(4,128)(2,1)} %copy.25), calls=%async_computation | async-start | bytes 2621440 | tf_op jit(solution)/shard_map/all_to_all | solution.py:50
  112.4 8.6 %collective-permute-start = (bf16[1,4,10,2048]{3,2,1,0:T(8,128)(2,1)S(1)}, bf16[1,4,10,2048]{3,2,1,0:T(8,128)(2,1)S(1)}, u32[]{:S(2)}, u32[]{:S(2)}) collective-permute-start(bf16[1,4,10,2048]{3,2,1,0:T(8,128)(2,1)S(1)} %get-tuple-element.11), channel_id=1, source_target_pairs={{0,2},{2,0},{4,6},{6,4},{8,10},{10,8},{12,14},{14,12},{1,3},{3,1},... | collective-permute-start | bytes 491528 | tf_op jit(solution)/shard_map/ppermute | solution.py:25
  114.0 17.1 %collective-permute-start.1 = (bf16[1,4,10,2048]{3,2,1,0:T(8,128)(2,1)S(1)}, bf16[1,4,10,2048]{3,2,1,0:T(8,128)(2,1)S(1)}, u32[]{:S(2)}, u32[]{:S(2)}) collective-permute-start(bf16[1,4,10,2048]{3,2,1,0:T(8,128)(2,1)S(1)} %get-tuple-element.10), channel_id=1, source_target_pairs={{0,4},{2,6},{4,0},{6,2},{8,12},{10,14},{12,8},{14,10},{1,5},{3,7},... | collective-permute-start | bytes 491528 | tf_op jit(solution)/shard_map/ppermute | solution.py:25
  115.5 20.3 %collective-permute-start.2 = (bf16[1,4,10,2048]{3,2,1,0:T(8,128)(2,1)S(1)}, bf16[1,4,10,2048]{3,2,1,0:T(8,128)(2,1)S(1)}, u32[]{:S(2)}, u32[]{:S(2)}) collective-permute-start(bf16[1,4,10,2048]{3,2,1,0:T(8,128)(2,1)S(1)} %get-tuple-element.9), channel_id=1, source_target_pairs={{0,6},{2,4},{4,2},{6,0},{8,14},{10,12},{12,10},{14,8},{1,7},{3,5},... | collective-permute-start | bytes 491528 | tf_op jit(solution)/shard_map/ppermute | solution.py:25
  116.0 19.7 %collective-permute-start.3 = (bf16[1,4,10,2048]{3,2,1,0:T(8,128)(2,1)S(1)}, bf16[1,4,10,2048]{3,2,1,0:T(8,128)(2,1)S(1)}, u32[]{:S(2)}, u32[]{:S(2)}) collective-permute-start(bf16[1,4,10,2048]{3,2,1,0:T(8,128)(2,1)S(1)} %get-tuple-element.8), channel_id=1, source_target_pairs={{0,8},{2,10},{4,12},{6,14},{8,0},{10,2},{12,4},{14,6},{1,9},{3,11}... | collective-permute-start | bytes 491528 | tf_op jit(solution)/shard_map/ppermute | solution.py:25
  116.2 34.8 %collective-permute-start.4 = (bf16[1,4,10,2048]{3,2,1,0:T(8,128)(2,1)S(1)}, bf16[1,4,10,2048]{3,2,1,0:T(8,128)(2,1)S(1)}, u32[]{:S(2)}, u32[]{:S(2)}) collective-permute-start(bf16[1,4,10,2048]{3,2,1,0:T(8,128)(2,1)S(1)} %get-tuple-element.7), channel_id=1, source_target_pairs={{0,10},{2,8},{4,14},{6,12},{8,2},{10,0},{12,6},{14,4},{1,11},{3,9}... | collective-permute-start | bytes 491528 | tf_op jit(solution)/shard_map/ppermute | solution.py:25
  121.0 38.8 %collective-permute-start.5 = (bf16[1,4,10,2048]{3,2,1,0:T(8,128)(2,1)S(1)}, bf16[1,4,10,2048]{3,2,1,0:T(8,128)(2,1)S(1)}, u32[]{:S(2)}, u32[]{:S(2)}) collective-permute-start(bf16[1,4,10,2048]{3,2,1,0:T(8,128)(2,1)S(1)} %get-tuple-element.6), channel_id=1, source_target_pairs={{0,12},{2,14},{4,8},{6,10},{8,4},{10,6},{12,0},{14,2},{1,13},{3,15... | collective-permute-start | bytes 491528 | tf_op jit(solution)/shard_map/ppermute | solution.py:25
  131.0 33.8 %collective-permute-start.6 = (bf16[1,4,10,2048]{3,2,1,0:T(8,128)(2,1)S(1)}, bf16[1,4,10,2048]{3,2,1,0:T(8,128)(2,1)S(1)}, u32[]{:S(2)}, u32[]{:S(2)}) collective-permute-start(bf16[1,4,10,2048]{3,2,1,0:T(8,128)(2,1)S(1)} %get-tuple-element.5), channel_id=1, source_target_pairs={{0,14},{2,12},{4,10},{6,8},{8,6},{10,4},{12,2},{14,0},{1,15},{3,13... | collective-permute-start | bytes 491528 | tf_op jit(solution)/shard_map/ppermute | solution.py:25
  164.9 4.5 %copy-start.1 = (bf16[128,2048]{1,0:T(8,128)(2,1)S(1)}, bf16[128,2048]{1,0:T(8,128)(2,1)}, u32[]{:S(2)}) copy-start(bf16[128,2048]{1,0:T(8,128)(2,1)} %param.6) | copy-start | bytes 1572868
Sparse Core Ops, SparseCore 0:
  8.9 38.9 all-gather.2
  49.4 38.7 all-gather.4
